TPU v7x, 128 devices: a whole 4x4x4 slice. The times are simulated.
128 devices in a mesh: tile: 16 (over x, z), depth: 8 (over y, core).
Axes of the slice: x: 4, y: 4, z: 4, core: 2. Of those that a mesh axis runs over, the one named last changes fastest.
Arguments:
- volume: float32 [512, 512, 1024], P('tile', 'depth')
- slab_place: int32 [8], replicated, may hold values from 0 to 7, each once
- control_index: int32 [8], replicated, may hold values from 0 to 255, as said below
- control_extinction: float32 [8], replicated, may hold values from 0.0001953125 to 0.01171875
- control_color: float32 [3, 8], replicated, may hold values from 0.2 to 1
Outputs:
- image: float32 [3, 512, 1024], P(None, 'tile', 'depth')
Inputs may be any that keep to these rules, and one draw needn't show every extreme that they name: `slab_place`: each view position is given to exactly one slab. `control_index`: strictly increasing; the first is 0 and the last is 255.
All inputs are finite; a program needn't handle non-finite values.
Results may differ from a plain program's by a relative error of at most 0.0003.
Values sent between devices are 32-bit elements; how exact they have to be, the bound alone decides.
A program may use at most 128 MiB of HBM per device.

v0:
```python
import jax
import jax.numpy as jnp
from jax import lax
from jax.sharding import PartitionSpec as P

TABLE = 256


def with_halo(block, sides, width):
    for axis, dim in sides:
        count = lax.axis_size(axis)
        forward = [(i, i + 1) for i in range(count - 1)]
        backward = [(target, source) for source, target in forward]
        low = lax.ppermute(
            lax.slice_in_dim(block, block.shape[dim] - width, None, axis=dim), axis, forward
        )
        high = lax.ppermute(lax.slice_in_dim(block, 0, width, axis=dim), axis, backward)
        block = jnp.concatenate([low, block, high], axis=dim)
    return block


def transfer(position, control_index, control_extinction, control_color):
    points = control_index.astype(jnp.float32)
    point_count = control_index.shape[0]
    extinct = jnp.zeros_like(position)
    emitted = [jnp.zeros_like(position) for channel in range(3)]
    for point in range(point_count):
        if point > 0:
            rising = (position - points[point - 1]) / (points[point] - points[point - 1])
        else:
            rising = jnp.ones_like(position)
        if point + 1 < point_count:
            falling = (points[point + 1] - position) / (points[point + 1] - points[point])
        else:
            falling = jnp.ones_like(position)
        hat_weight = jnp.maximum(0.0, jnp.minimum(rising, falling))
        extinct = extinct + hat_weight * control_extinction[point]
        emitted = [
            emitted[channel] + hat_weight * control_color[channel, point] for channel in range(3)
        ]
    return (extinct, emitted)


def shade_slab(
    rows_padded,
    front_plane,
    back_plane,
    low_value,
    high_value,
    control_index,
    control_extinction,
    control_color,
):
    center = rows_padded[1:-1]
    grad_rows = 0.5 * (rows_padded[2:] - rows_padded[:-2])
    deepened = jnp.concatenate([front_plane[:, None], center, back_plane[:, None]], axis=1)
    grad_depth = 0.5 * (deepened[:, 2:] - deepened[:, :-2])
    widened = jnp.pad(center, ((0, 0), (0, 0), (1, 1)))
    grad_cols = 0.5 * (widened[:, :, 2:] - widened[:, :, :-2])
    facing = 0.48 * grad_rows + 0.6 * grad_depth + 0.64 * grad_cols
    shading = 0.3 + 0.7 * jnp.abs(facing) * lax.rsqrt(
        grad_rows * grad_rows + grad_depth * grad_depth + grad_cols * grad_cols + 1.0
    )
    position = (center - low_value) / (high_value - low_value + 1.0) * (TABLE - 1.0)
    extinct, emitted = transfer(position, control_index, control_extinction, control_color)
    opacity = 1.0 - jnp.exp(-extinct)
    plane_ids = jnp.arange(center.shape[1], dtype=jnp.int32)
    earlier_mask = (plane_ids[:, None] > plane_ids[None, :]).astype(jnp.float32)
    optical = jnp.einsum("zy,ryc->rzc", earlier_mask, extinct, precision=lax.Precision.HIGHEST)
    contrib = jnp.exp(-optical) * opacity * shading
    colors = jnp.stack(
        [jnp.sum(contrib * emitted[channel], axis=1) for channel in range(3)], axis=0
    )
    transmit = jnp.exp(-jnp.sum(extinct, axis=1))
    return (colors, transmit)


def body(volume, slab_place, control_index, control_extinction, control_color):
    rows, planes, cols = volume.shape
    extremes = lax.pmax((jnp.max(volume), -jnp.min(volume)), ("tile", "depth"))
    high_value = extremes[0]
    low_value = -extremes[1]
    slots = lax.axis_size("depth")
    my_index = lax.axis_index("depth")
    slot_ids = jnp.arange(slots, dtype=jnp.int32)
    my_place = jnp.sum(jnp.where(slot_ids == my_index, slab_place, 0))
    faces = jnp.stack([volume[:, 0], volume[:, -1]], axis=0)
    every_face = lax.all_gather(faces, "depth", axis=0, tiled=True).reshape(slots, 2, rows, cols)
    before = (slab_place == my_place - 1).astype(jnp.float32)
    after = (slab_place == my_place + 1).astype(jnp.float32)
    front_plane = jnp.sum(before[:, None, None] * every_face[:, 1], axis=0)
    back_plane = jnp.sum(after[:, None, None] * every_face[:, 0], axis=0)
    rows_padded = with_halo(volume, (("tile", 0),), 1)
    colors, transmit = shade_slab(
        rows_padded,
        front_plane,
        back_plane,
        low_value,
        high_value,
        control_index,
        control_extinction,
        control_color,
    )
    every_transmit = lax.all_gather(transmit[None], "depth", axis=0, tiled=True)
    ahead_mask = slab_place < my_place
    front_product = jnp.prod(jnp.where(ahead_mask[:, None, None], every_transmit, 1.0), axis=0)
    image = lax.psum_scatter(front_product[None] * colors, "depth", scatter_dimension=2, tiled=True)
    return image


def solution(mesh):
    placed = (P("tile", "depth", None), P(), P(), P(), P())
    return jax.shard_map(
        body, mesh=mesh, in_specs=placed, out_specs=P(None, "tile", "depth"), check_vma=False
    )
```

profile of v0, /device:TPU:1, one launch (start us, length us, event | category | flops | bytes accessed | tf_op | source)
XLA Modules:
  0.0 364.7 jit_solution(7676726017657937103)
XLA Ops:
  6.5 0.0 copy-start.2
  6.5 0.0 all-gather.6.cloned.1.call-start
  6.5 0.7 convert_element_type.12
  7.2 6.1 %fusion.12 = (f32[]{:T(128)}, f32[]{:T(128)}) fusion(f32[32,64,1024]{2,1,0:T(8,128)} %param.5), kind=kLoop, calls=%fused_computation.44 | loop fusion | flops 4194302 | bytes 8388616 | tf_op jit(solution)/shard_map/reduce_min | solution.py:80
  14.0 68.8 %all-reduce.1 = (f32[]{:T(128)}, f32[]{:T(128)}) all-reduce(f32[]{:T(128)} %get-tuple-element.6, f32[]{:T(128)S(6)} %neg.24), channel_id=1, replica_groups=mesh['tile'=16,'depth'=8] {'tile','depth'}, use_global_device_ids=true, to_apply=%region_4.5 | all-reduce | flops 2 | bytes 16 | tf_op jit(solution)/shard_map/pmax | solution.py:80
  83.4 0.7 fusion.19
  92.7 0.0 copy-done.2
  92.7 0.7 fusion.18
  94.1 0.0 copy-start.3
  94.1 0.0 copy-start.1
  94.1 28.8 %fusion.13 = (f32[32,1024]{1,0:T(8,128)S(1)}, f32[32,64,1024]{2,1,0:T(8,128)}) fusion(f32[]{:T(128)} %bitcast.15, f32[]{:T(128)} %bitcast.14, f32[]{:T(128)S(6)} %sub.154, f32[]{:T(128)} %bitcast.13, f32[]{:T(128)} %bitcast.12, f32[]{:T(128)S(6)} %sub.150, f32[]{:T(128)} %bitcast.11, f32[]{:T(128)} %bitcast.10, f32[]{:T(128)S(6)} %sub.146, f32[]{:T(128)} %bitcast.9, ...), kind=kLoop, calls=%fused_computation.45 | loop fusion | flops 127893504 | bytes 16908388 | tf_op jit(solution)/shard_map/reduce_sum | solution.py:74
  122.9 0.7 negate_exponential_fusion
  123.5 0.0 all-gather.6.cloned.1.call-update
  123.5 0.0 all-gather.4.cloned.1.call-start
  123.6 1.8 fusion.15
  125.4 0.1 copy_bitcast_fusion
  125.4 0.7 pad_maximum_fusion.4
  126.1 0.0 all-gather.4.cloned.1.call-update
  126.2 0.0 reduce-scatter.2.cloned.1.call-start
  126.2 1.1 fusion.14
  127.3 1.3 collective-permute-start
  128.6 4.2 %collective-permute-start.1 = (f32[1,64,1024]{2,1,0:T(8,128)S(1)}, f32[1,64,1024]{2,1,0:T(8,128)S(1)}, u32[]{:S(2)}, u32[]{:S(2)}) collective-permute-start(f32[1,64,1024]{2,1,0:T(8,128)S(1)} %get-tuple-element.14), channel_id=1, source_target_pairs={{0,8},{8,16},{16,24},{24,32},{32,40},{40,48},{48,56},{56,64},{64,7... | collective-permute-start | bytes 786440 | tf_op jit(solution)/shard_map/ppermute | solution.py:14
  132.8 0.0 copy-done.3
  132.8 0.7 fusion.11
  134.7 0.0 copy-done.1
  134.7 0.7 fusion.17
  135.4 0.7 fusion.16
  136.1 0.6 broadcast_compare_fusion
  136.8 7.1 %all-gather.6.cloned.1.call-done = f32[256,1024]{1,0:T(8,128)} async-done(((f32[32,1024]{1,0:T(8,128)}), f32[256,1024]{1,0:T(8,128)}) %all-gather.6.cloned.1.call-update) | async-done | bytes 1048592 | tf_op jit(solution)/shard_map/all_gather | solution.py:104
  143.9 2.0 select_reduce_fusion
  145.9 24.7 %all-gather.4.cloned.1.call-done = f32[16,32,1024]{2,1,0:T(8,128)} async-done(((f32[2,32,1024]{2,1,0:T(8,128)}), f32[16,32,1024]{2,1,0:T(8,128)}) %all-gather.4.cloned.1.call-update) | async-done | bytes 2097168 | tf_op jit(solution)/shard_map/all_gather | solution.py:88
  170.7 1.9 fusion.7
  172.5 0.1 broadcast_in_dim.32
  172.6 0.1 broadcast_in_dim.33
  172.7 0.0 collective-permute-done
  172.7 0.0 collective-permute-done.1
  172.7 62.3 %multiply_reduce_fusion = (f32[32,1024]{1,0:T(8,128)S(1)}, f32[32,1024,64]{1,2,0:T(8,128)}) fusion(f32[]{:T(128)} %bitcast.49, f32[]{:T(128)} %bitcast.48, f32[]{:T(128)} %bitcast.47, f32[]{:T(128)} %bitcast.46, f32[]{:T(128)} %bitcast.45, f32[]{:T(128)} %bitcast.44, f32[]{:T(128)} %bitcast.43, f32[]{:T(128)} %bitcast.42, f32[32,64,1024]{2,1,0:T(8,128)} %param.5, ...), kind=kOutput, calls=%fused_computation.11 | convolution fusion | flops 1803522048 | bytes 34480164 | tf_op jit(solution)/shard_map/zy,ryc->rzc/dot_general | solution.py:69
  235.0 47.1 %multiply_reduce_fusion.1 = f32[32,1024]{1,0:T(8,128)S(1)} fusion(f32[]{:T(128)} %bitcast.40, f32[]{:T(128)} %bitcast.39, f32[]{:T(128)} %bitcast.38, f32[]{:T(128)} %bitcast.37, f32[]{:T(128)} %bitcast.36, f32[]{:T(128)} %bitcast.35, f32[]{:T(128)} %bitcast.34, f32[]{:T(128)} %bitcast.33, f32[32,64,1024]{2,1,0:T(8,128)} %param.5, ...), kind=kLoop, calls=%fused_computation.12 | loop fusion | flops 192905216 | bytes 26083428 | tf_op jit(solution)/shard_map/reduce_sum | solution.py:72
  282.2 0.0 copy-start
  282.2 47.1 %multiply_reduce_fusion.2 = f32[32,1024]{1,0:T(8,128)S(1)} fusion(f32[]{:T(128)} %bitcast.31, f32[]{:T(128)} %bitcast.30, f32[]{:T(128)} %bitcast.29, f32[]{:T(128)} %bitcast.28, f32[]{:T(128)} %bitcast.27, f32[]{:T(128)} %bitcast.26, f32[]{:T(128)} %bitcast.25, f32[]{:T(128)} %bitcast.24, f32[32,64,1024]{2,1,0:T(8,128)} %param.5, ...), kind=kLoop, calls=%fused_computation.13 | loop fusion | flops 192905216 | bytes 26083428 | tf_op jit(solution)/shard_map/reduce_sum | solution.py:72
  329.3 0.0 copy-done
  329.3 0.8 maximum_multiply_fusion
  330.1 0.0 reduce-scatter.2.cloned.1.call-update
  330.1 28.1 %reduce-scatter.2.cloned.1.call-done = f32[3,32,128]{2,1,0:T(8,128)} async-done(((f32[3,32,1024]{2,1,0:T(8,128)}), f32[3,32,128]{2,1,0:T(8,128)}) %reduce-scatter.2.cloned.1.call-update) | async-done | bytes 49168 | tf_op jit(solution)/shard_map/reduce_scatter | solution.py:107
Async XLA Ops:
  6.5 86.1 %copy-start.2 = (f32[8]{0:T(128)S(1)}, f32[8]{0:T(128)}, u32[]{:S(2)}) copy-start(f32[8]{0:T(128)} %param.8) | copy-start | bytes 100
  6.5 137.4 %all-gather.6.cloned.1.call-start = ((), (), s32[]{:S(2)}) async-start(), calls=%async_computation.3 | async-start | bytes 1179648 | tf_op jit(solution)/shard_map/all_gather | solution.py:104
  94.1 38.7 %copy-start.3 = (s32[8]{0:T(128)S(1)}, s32[8]{0:T(128)}, u32[]{:S(2)}) copy-start(s32[8]{0:T(128)} %param.6) | copy-start | bytes 100
  94.1 40.7 %copy-start.1 = (f32[3,8]{1,0:T(4,128)S(1)}, f32[3,8]{1,0:T(4,128)}, u32[]{:S(2)}) copy-start(f32[3,8]{1,0:T(4,128)} %param.9) | copy-start | bytes 292
  123.5 47.1 %all-gather.4.cloned.1.call-start = ((), (), s32[]{:S(2)}) async-start(), calls=%async_computation.1 | async-start | bytes 2359296 | tf_op jit(solution)/shard_map/all_gather | solution.py:88
  126.2 232.0 %reduce-scatter.2.cloned.1.call-start = ((), (), s32[]{:S(2)}) async-start(), calls=%async_computation.2 | async-start | bytes 442368 | tf_op jit(solution)/shard_map/reduce_scatter | solution.py:107
  127.3 45.4 %collective-permute-start = (f32[1,64,1024]{2,1,0:T(8,128)S(1)}, f32[1,64,1024]{2,1,0:T(8,128)S(1)}, u32[]{:S(2)}, u32[]{:S(2)}) collective-permute-start(f32[1,64,1024]{2,1,0:T(8,128)S(1)} %get-tuple-element.13), channel_id=1, source_target_pairs={{8,0},{16,8},{24,16},{32,24},{40,32},{48,40},{56,48},{64,56},{72,6... | collective-permute-start | bytes 786440 | tf_op jit(solution)/shard_map/ppermute | solution.py:17
  128.6 44.1 %collective-permute-start.1 = (f32[1,64,1024]{2,1,0:T(8,128)S(1)}, f32[1,64,1024]{2,1,0:T(8,128)S(1)}, u32[]{:S(2)}, u32[]{:S(2)}) collective-permute-start(f32[1,64,1024]{2,1,0:T(8,128)S(1)} %get-tuple-element.14), channel_id=1, source_target_pairs={{0,8},{8,16},{16,24},{24,32},{32,40},{40,48},{48,56},{56,64},{64,7... | collective-permute-start | bytes 786440 | tf_op jit(solution)/shard_map/ppermute | solution.py:14
  282.2 47.2 %copy-start = (f32[32,1024]{1,0:T(8,128)S(1)}, f32[32,1024]{1,0:T(8,128)}, u32[]{:S(2)}) copy-start(f32[32,1024]{1,0:T(8,128)} %select_reduce_fusion) | copy-start | bytes 393220
Sparse Core Ops, SparseCore 0:
  123.7 20.1 all-gather.5
  145.6 25.0 all-gather.3
  330.2 27.9 reduce-scatter.1
where the time goes:
time: 368 us; the launch traced here: 365 us
  other arithmetic  137 us (37%)
  blocking collectives  68.8 us (19%)
  matrix products  62.3 us (17%)
  waiting for transfers between devices  60 us (16%)
  between operations  25.1 us (7%)
  local copies, waits for them, and re-layouts  5.81 us (2%)
  starting transfers between devices  5.56 us (2%)
    reduce_sum x2, other arithmetic, shade_slab(): jnp.sum(contrib * emitted[channel], axis=1)  94.3 us
    pmax x1, blocking collectives, body(): extremes = lax.pmax((jnp.max(volume), -jnp.min(volume)), ('tile', 'depth'))  68.8 us
    dot_general x1, matrix products, shade_slab(): jnp.einsum('zy,ryc->rzc', earlier_mask, extinct, precision=lax.Precision....  62.3 us
    reduce_sum x1, other arithmetic, shade_slab(): transmit = jnp.exp(-jnp.sum(extinct, axis=1))  28.8 us
    reduce_scatter x1, waiting for transfers between devices, body(): lax.psum_scatter(front_product[None] * colors, 'depth', scatter_dimension...  28.1 us
    all_gather x1, waiting for transfers between devices, body(): lax.all_gather(faces, 'depth', axis=0, tiled=True)  24.7 us
  transfers between devices with their start and end apart: 5, of which 3 were waited for; matrix products, arithmetic and copies ran while one was open for 3% of the time, Pallas kernels for 0%

commit v1 on v0

v1 whole, which is shorter than its diff:
```python
import functools

import jax
import jax.numpy as jnp
import numpy as np
from jax import lax
from jax.experimental import pallas as pl
from jax.experimental.pallas import tpu as pltpu
from jax.sharding import PartitionSpec as P

MESH = pl.DeviceIdType.MESH
TABLE = 256
LANES = 128
SUB = 8
PITCH = 8
KA, KB, KC = 0.48 / 0.64, 0.6 / 0.64, 0.7 * 0.64
BASE = 0.3 / KC
LOG2E = float(np.log2(np.e))
BIG = 3.0e38


def full(value):
    return jnp.full((SUB, LANES), value, jnp.float32)


def lookup(table, index):
    dims = lax.GatherDimensionNumbers(
        offset_dims=(),
        collapsed_slice_dims=(0,),
        start_index_map=(0,),
        operand_batching_dims=(1,),
        start_indices_batching_dims=(1,),
    )
    return lax.gather(
        table, index[..., None], dims, (1, 1), mode=lax.GatherScatterMode.PROMISE_IN_BOUNDS
    )


def shade(row_diff, plane_diff, col_diff):
    facing = (col_diff + KB * plane_diff) + KA * row_diff
    norm = (row_diff * row_diff + plane_diff * plane_diff) + (col_diff * col_diff + 1.0)
    return BASE + jnp.abs(facing) * lax.rsqrt(norm)


def col_diffs(tiles, lane):
    right = [pltpu.roll(x, 1, 1) for x in tiles]
    left = [pltpu.roll(x, LANES - 1, 1) for x in tiles]
    zero = jnp.zeros((SUB, LANES), jnp.float32)
    last = len(tiles) - 1
    out = []
    for c in range(len(tiles)):
        prev = jnp.where(lane == 0, right[c - 1] if c else zero, right[c])
        nxt = jnp.where(lane == LANES - 1, left[c + 1] if c < last else zero, left[c])
        out.append(nxt - prev)
    return out


def kernel(
    dims,
    volume,
    place_hbm,
    index_hbm,
    extinct_hbm,
    color_hbm,
    out,
    vol,
    shaded,
    face_in,
    face_out,
    face,
    part1,
    part2,
    packed,
    gathered,
    place,
    index,
    extinct,
    color,
    slots,
    param_sem,
    load_sem,
    halo_send,
    halo_recv,
    f1_send,
    f1_recv,
    f2_send,
    f2_recv,
    m1_send,
    m1_recv,
    m2_send,
    m2_recv,
    out_send,
    out_recv,
):
    tiles_n, slabs, rows, planes, cols = dims
    ct = cols // LANES
    blocks = rows // SUB
    me = lax.axis_index("depth")
    tile = lax.axis_index("tile")
    below = lax.rem(tile + 1, tiles_n)
    above = lax.rem(tile + tiles_n - 1, tiles_n)

    def depth_peer(j):
        return lax.rem(me + j, slabs)

    def tile_peer(j):
        return lax.rem(tile + j, tiles_n)

    params = [
        pltpu.make_async_copy(src, dst, param_sem.at[i])
        for i, (src, dst) in enumerate(
            ((place_hbm, place), (index_hbm, index), (extinct_hbm, extinct), (color_hbm, color))
        )
    ]
    for copy in params:
        copy.start()

    def columns(c):
        return pl.ds(pl.multiple_of(c * LANES, LANES), LANES)

    def load(c):
        return pltpu.make_async_copy(
            volume.at[:, :, columns(c)],
            vol.at[c, pl.ds(1, rows), pl.ds(0, planes), :],
            load_sem.at[c],
        )

    for c in range(ct):
        load(c).start()

    barrier = pltpu.get_barrier_semaphore()
    for j in range(1, slabs):
        pl.semaphore_signal(
            barrier, inc=1, device_id={"depth": depth_peer(j)}, device_id_type=MESH
        )
    for j in range(1, tiles_n):
        pl.semaphore_signal(barrier, inc=1, device_id={"tile": tile_peer(j)}, device_id_type=MESH)

    for copy in params:
        copy.wait()
    slots[0] = slabs
    slots[slabs + 1] = slabs
    for p in range(slabs):
        found = jnp.int32(0)
        for s in range(slabs):
            found = jnp.where(place[s] == p, jnp.int32(s), found)
        slots[p + 1] = lax.rem(me - found + slabs, slabs)
    zero = jnp.zeros((SUB, LANES), jnp.float32)
    for side in range(2):
        for b in range(blocks):
            face_in[slabs, side, pl.ds(b * SUB, SUB), :] = zero

    pl.semaphore_wait(barrier, slabs - 1 + tiles_n - 1)

    def halo(side, c):
        row = rows - 1 if side == 0 else 0
        return pltpu.make_async_remote_copy(
            src_ref=volume.at[row, :, columns(c)],
            dst_ref=vol.at[c, rows + 1 if side else 0, pl.ds(0, planes), :],
            send_sem=halo_send.at[side, c],
            recv_sem=halo_recv.at[side, c],
            device_id={"tile": above if side else below},
            device_id_type=MESH,
        )

    def face_first(j, side):
        owner = depth_peer(j)
        src = volume.at[
            :, side * (planes - 1), columns(owner)
        ]
        if j == 0:
            return pltpu.make_async_copy(src, face_in.at[0, side], f1_send.at[0, side])
        return pltpu.make_async_remote_copy(
            src_ref=src,
            dst_ref=face_in.at[j, side],
            send_sem=f1_send.at[j, side],
            recv_sem=f1_recv.at[j, side],
            device_id={"depth": owner},
            device_id_type=MESH,
        )

    def face_second(j):
        return pltpu.make_async_remote_copy(
            src_ref=face_out.at[j],
            dst_ref=face.at[me],
            send_sem=f2_send.at[j],
            recv_sem=f2_recv.at[j],
            device_id={"depth": depth_peer(j)},
            device_id_type=MESH,
        )

    for j in range(slabs):
        for side in range(2):
            face_first(j, side).start()

    @pl.when(tile < tiles_n - 1)
    def _():
        for c in range(ct):
            halo(0, c).start()

    @pl.when(tile > 0)
    def _():
        for c in range(ct):
            halo(1, c).start()

    pieces = planes // SUB

    def extremes_block(c, carry):
        load(c).wait()

        def step(r, carry):
            high, low = carry
            new_high, new_low = [], []
            for q in range(pieces):
                at = vol.at[c, r + 1, pl.ds(q * SUB, SUB), :]
                half = at[...] * 0.5
                at[...] = half
                new_high.append(jnp.maximum(high[q], half))
                new_low.append(jnp.minimum(low[q], half))
            return tuple(new_high), tuple(new_low)

        return lax.fori_loop(0, rows, step, carry, unroll=4)

    start = (tuple([full(-BIG)] * pieces), tuple([full(BIG)] * pieces))
    high, low = lax.fori_loop(0, ct, extremes_block, start)
    part1[0, 0:1, :] = jnp.max(functools.reduce(jnp.maximum, high), axis=0, keepdims=True)
    part1[0, 1:2, :] = -jnp.min(functools.reduce(jnp.minimum, low), axis=0, keepdims=True)

    def part_copy(stage, j):
        buf, send, recv = (part1, m1_send, m1_recv) if stage == 1 else (part2, m2_send, m2_recv)
        peer = {"depth": depth_peer(j)} if stage == 1 else {"tile": tile_peer(j)}
        return pltpu.make_async_remote_copy(
            src_ref=buf.at[0],
            dst_ref=buf.at[j],
            send_sem=send.at[j],
            recv_sem=recv.at[j],
            device_id=peer,
            device_id_type=MESH,
        )

    for j in range(1, slabs):
        part_copy(1, j).start()

    for j in range(slabs):
        for side in range(2):
            if j == 0:
                face_first(j, side).wait()
            else:
                face_first(j, side).wait_recv()
    for j in range(slabs):
        at = place[depth_peer(j)]
        front = slots[at]
        back = slots[at + 2]
        for b in range(blocks):
            rs = pl.ds(b * SUB, SUB)
            front_value = face_in[front, 1, rs, :] * 0.5
            back_value = face_in[back, 0, rs, :] * 0.5
            if j == 0:
                face[me, 0, rs, :] = front_value
                face[me, 1, rs, :] = back_value
            else:
                face_out[j, 0, rs, :] = front_value
                face_out[j, 1, rs, :] = back_value
        if j:
            face_second(j).start()

    pitch = planes + PITCH
    flat = vol.reshape(ct, (rows + 2) * pitch, LANES)

    def view(p, c, b, shift):
        return flat[c, pl.ds((b * SUB + 1 + shift) * pitch + p, SUB, stride=pitch), :]

    lane = lax.broadcasted_iota(jnp.int32, (SUB, LANES), 1)
    sub = lax.broadcasted_iota(jnp.int32, (SUB, LANES), 0)

    def shade_block(b):
        def step(i, carry):
            p = i + 1
            prev, here = carry[:ct], carry[ct:]
            nxt = tuple(view(p + 1, c, b, 0) for c in range(ct))
            diffs = col_diffs(here, lane)
            for c in range(ct):
                shaded[b, c, p] = shade(
                    view(p, c, b, 1) - view(p, c, b, -1), nxt[c] - prev[c], diffs[c]
                )
            return tuple(here) + nxt

        first = tuple(view(p, c, b, 0) for p in range(2) for c in range(ct))
        lax.fori_loop(0, planes - 2, step, first, unroll=31)

    def inner(i, _):
        shade_block(i + 1)
        return 0

    lax.fori_loop(0, 1, inner, 0)

    for j in range(1, slabs):
        part_copy(1, j).wait_recv()
    part2[0] = jnp.max(part1[...], axis=0)
    for j in range(1, tiles_n):
        part_copy(2, j).start()

    lax.fori_loop(1, blocks - 2, inner, 0)

    def halo_row(side, scale):
        def step(c, _):
            if scale:
                halo(side, c).wait_recv()
            for q in range(pieces):
                at = vol.at[c, rows + 1 if side else 0, pl.ds(q * SUB, SUB), :]
                at[...] = at[...] * 0.5 if scale else zero
            return 0

        lax.fori_loop(0, ct, step, 0)

    @pl.when(tile > 0)
    def _():
        halo_row(0, True)

    @pl.when(tile == 0)
    def _():
        halo_row(0, False)

    @pl.when(tile < tiles_n - 1)
    def _():
        halo_row(1, True)

    @pl.when(tile == tiles_n - 1)
    def _():
        halo_row(1, False)

    def outer(i, _):
        shade_block(i * (blocks - 1))
        return 0

    lax.fori_loop(0, 2, outer, 0)

    for j in range(1, slabs):
        face_second(j).wait_recv()

    def edge_planes(b, _):
        rs = pl.ds(pl.multiple_of(b * SUB, SUB), SUB)
        for side in range(2):
            p = side * (planes - 1)
            diffs = col_diffs([view(p, c, b, 0) for c in range(ct)], lane)
            for c in range(ct):
                other = face[c, side, rs, :]
                if side == 0:
                    plane_diff = view(1, c, b, 0) - other
                else:
                    plane_diff = other - view(planes - 2, c, b, 0)
                shaded[b, c, p] = shade(view(p, c, b, 1) - view(p, c, b, -1), plane_diff, diffs[c])
        return 0

    lax.fori_loop(0, blocks, edge_planes, 0)

    def by_segment(values):
        table = full(values[0])
        for s in range(1, len(values)):
            table = jnp.where(sub == s, values[s], table)
        return table

    knots = index.shape[0]
    points = [index[k].astype(jnp.float32) for k in range(knots)]
    lower = by_segment(points[:-1])
    upper = by_segment(points[1:])
    width = jnp.where(sub < knots - 1, upper - lower, 1.0)
    offsets, slopes = [], []
    for channel in range(4):
        scale = -LOG2E if channel == 0 else KC
        values = [
            extinct[k] if channel == 0 else color[channel - 1, k] for k in range(knots)
        ]
        begin, end = by_segment(values[:-1]), by_segment(values[1:])
        slope = (end - begin) / width
        offsets.append((begin - slope * lower) * scale)
        slopes.append(slope * scale)

    for j in range(1, tiles_n):
        part_copy(2, j).wait_recv()
    extremes = jnp.max(jnp.max(part2[...], axis=0), axis=1, keepdims=True)
    extremes = jnp.broadcast_to(extremes, (2, LANES))
    low_value = jnp.broadcast_to(-extremes[1:2, :], (SUB, LANES))
    span = jnp.broadcast_to(extremes[0:1, :] + extremes[1:2, :], (SUB, LANES)) + 0.5
    unit = span * (1.0 / (TABLE - 1.0))
    slopes = [slope * ((TABLE - 1.0) / span) for slope in slopes]
    bounds = [points[k] * unit for k in range(1, knots - 1)]
    odd = jnp.where(sub >= 6, BIG, jnp.where(sub >= 4, bounds[4], jnp.where(sub >= 2, bounds[2], bounds[0])))

    group = 2

    def render_block(b, _):
        def render_group(g, _):
            def step(p, carry):
                out_carry = []
                for k in range(group):
                    through, sums = carry[k]
                    c = g * group + k
                    dist = view(p, c, b, 0) - low_value
                    even = jnp.where(dist >= bounds[1], 2, 0)
                    even = jnp.where(dist >= bounds[3], 4, even)
                    even = jnp.where(dist >= bounds[5], 6, even)
                    segment = jnp.where(dist >= lookup(odd, even), even + 1, even)
                    offset = [lookup(t, segment) for t in offsets]
                    slope = [lookup(t, segment) for t in slopes]
                    rest = through * jnp.exp2(offset[0] + slope[0] * dist)
                    weight = (through - rest) * shaded[b, c, p]
                    sums = tuple(
                        sums[i] + weight * (offset[i + 1] + slope[i + 1] * dist) for i in range(3)
                    )
                    out_carry.append((rest, sums))
                return tuple(out_carry)

            begin = tuple((full(1.0), (full(0.0),) * 3) for _ in range(group))
            done = lax.fori_loop(0, planes, step, begin, unroll=16)
            for k in range(group):
                at = columns(g * group + k)
                for i in range(3):
                    packed[b, i, :, at] = done[k][1][i]
                packed[b, 3, :, at] = done[k][0]
            return 0

        lax.fori_loop(0, ct // group, render_group, 0)
        for j in range(1, slabs):
            result_copy(b, j).start()
        mine = columns(me)
        for i in range(4):
            gathered[b, 0, i] = packed[b, i, :, mine]
        return 0

    def result_copy(b, j):
        peer = depth_peer(j)
        return pltpu.make_async_remote_copy(
            src_ref=packed.at[b, :, :, columns(peer)],
            dst_ref=gathered.at[b, j],
            send_sem=out_send.at[b, j],
            recv_sem=out_recv.at[b, j],
            device_id={"depth": peer},
            device_id_type=MESH,
        )

    lax.fori_loop(0, blocks, render_block, 0)

    def arrive(b, _):
        for j in range(1, slabs):
            result_copy(b, j).wait_recv()
        return 0

    lax.fori_loop(0, blocks, arrive, 0)

    def composite(b, _):
        rs = pl.ds(pl.multiple_of(b * SUB, SUB), SUB)
        through = full(1.0)
        sums = [full(0.0)] * 3
        for p in range(slabs):
            slot = slots[p + 1]
            for i in range(3):
                sums[i] = sums[i] + through * gathered[b, slot, i]
            through = through * gathered[b, slot, 3]
        for i in range(3):
            out[i, rs, :] = sums[i]
        return 0

    lax.fori_loop(0, blocks, composite, 0)

    @pl.when(tile < tiles_n - 1)
    def _():
        for c in range(ct):
            halo(0, c).wait_send()

    @pl.when(tile > 0)
    def _():
        for c in range(ct):
            halo(1, c).wait_send()

    for j in range(1, slabs):
        for side in range(2):
            face_first(j, side).wait_send()
        face_second(j).wait_send()
        part_copy(1, j).wait_send()
    for j in range(1, tiles_n):
        part_copy(2, j).wait_send()

    def drain(b, _):
        for j in range(1, slabs):
            result_copy(b, j).wait_send()
        return 0

    lax.fori_loop(0, blocks, drain, 0)


def solution(mesh):
    tiles_n, slabs = mesh.shape["tile"], mesh.shape["depth"]

    def body(volume, slab_place, control_index, control_extinction, control_color):
        rows, planes, cols = volume.shape
        ct, blocks = cols // LANES, rows // SUB
        dims = (tiles_n, slabs, rows, planes, cols)
        f32, dma = jnp.float32, pltpu.SemaphoreType.DMA
        return pl.pallas_call(
            functools.partial(kernel, dims),
            out_shape=jax.ShapeDtypeStruct((3, rows, cols // slabs), f32),
            in_specs=[pl.BlockSpec(memory_space=pl.ANY)] * 5,
            out_specs=pl.BlockSpec(memory_space=pltpu.VMEM),
            scratch_shapes=[
                pltpu.VMEM((ct, rows + 2, planes + PITCH, LANES), f32),
                pltpu.VMEM((blocks, ct, planes, SUB, LANES), f32),
                pltpu.VMEM((slabs + 1, 2, rows, LANES), f32),
                pltpu.VMEM((slabs, 2, rows, LANES), f32),
                pltpu.VMEM((slabs, 2, rows, LANES), f32),
                pltpu.VMEM((slabs, 2, LANES), f32),
                pltpu.VMEM((tiles_n, 2, LANES), f32),
                pltpu.VMEM((blocks, 4, SUB, cols), f32),
                pltpu.VMEM((blocks, slabs, 4, SUB, LANES), f32),
                pltpu.SMEM(slab_place.shape, jnp.int32),
                pltpu.SMEM(control_index.shape, jnp.int32),
                pltpu.SMEM(control_extinction.shape, f32),
                pltpu.SMEM(control_color.shape, f32),
                pltpu.SMEM((slabs + 2,), jnp.int32),
                dma((4,)),
                dma((ct,)),
                dma((2, ct)),
                dma((2, ct)),
                dma((slabs, 2)),
                dma((slabs, 2)),
                dma((slabs,)),
                dma((slabs,)),
                dma((slabs,)),
                dma((slabs,)),
                dma((tiles_n,)),
                dma((tiles_n,)),
                dma((blocks, slabs)),
                dma((blocks, slabs)),
            ],
            compiler_params=pltpu.CompilerParams(
                collective_id=0, has_side_effects=True, vmem_limit_bytes=48 << 20
            ),
            name="render",
        )(volume, slab_place, control_index, control_extinction, control_color)

    placed = (P("tile", "depth", None), P(), P(), P(), P())
    return jax.shard_map(
        body, mesh=mesh, in_specs=placed, out_specs=P(None, "tile", "depth"), check_vma=False
    )
```

time: 368 us -> 42.7 us (0.12)
  other arithmetic: 137 us -> 0 us
  blocking collectives: 68.8 us -> 0 us
  matrix products: 62.3 us -> 0 us
  waiting for transfers between devices: 60 us -> 0 us
  Pallas kernels: 0 us -> 39.3 us
  between operations: 25.1 us -> 0.01 us
  starting transfers between devices: 5.56 us -> 0 us
    reduce_sum x5 -> x0, other arithmetic: 126 us -> none  [the longest x2 94.3 us: shade_slab(): jnp.sum(contrib * emitted[channel], axis=1)]
    pmax x1 -> x0, blocking collectives: 68.8 us -> none  [body(): extremes = lax.pmax((jnp.max(volume), -jnp.min(volume)), ('tile', 'depth'))]
    dot_general x1 -> x0, matrix products: 62.3 us -> none  [shade_slab(): jnp.einsum('zy,ryc->rzc', earlier_mask, extinct, precision=lax.Precision....]
    pallas_call x0 -> x1, Pallas kernels: none -> 39.3 us  [body(): pl.pallas_call(functools.partial(kernel, dims), out_shape=jax.ShapeDtypeS...]
    all_gather x2 -> x0, waiting for transfers between devices: 31.9 us -> none  [the longest x1 24.7 us: body(): lax.all_gather(faces, 'depth', axis=0, tiled=True)]
    reduce_scatter x1 -> x0, waiting for transfers between devices: 28.1 us -> none  [body(): lax.psum_scatter(front_product[None] * colors, 'depth', scatter_dimension...]
    reduce_min x1 -> x0, other arithmetic: 6.14 us -> none  [body(): extremes = lax.pmax((jnp.max(volume), -jnp.min(volume)), ('tile', 'depth'))]
    slice x6 -> x0, local copies, waits for them, and re-layouts: 5.55 us -> none  [the longest x1 1.76 us: body(): faces = jnp.stack([volume[:, 0], volume[:, -1]], axis=0)]
  transfers between devices with their start and end apart: 5 -> 0, of which waited for: 3 -> 0; matrix products, arithmetic and copies ran while one was open for 3% -> 0% of each run, Pallas kernels for 0% -> 0%
where the time goes in v1:
time: 42.7 us; the launch traced here: 42.5 us
  Pallas kernels  39.3 us (92%)
  local copies, waits for them, and re-layouts  3.27 us (8%)
    pallas_call x1, Pallas kernels, body(): pl.pallas_call(functools.partial(kernel, dims), out_shape=jax.ShapeDtypeS...  39.3 us
    unnamed x9, local copies, waits for them, and re-layouts  3.27 us

profile of v1, /device:TPU:1, one launch (start us, length us, event | category | flops | bytes accessed | tf_op | source)
XLA Modules:
  0.0 42.5 jit_solution(14349248438255767480)
XLA Ops:
  0.0 0.0 copy-start
  0.0 0.7 %copy-done = f32[3,8]{1,0:T(4,128)S(1)} copy-done((f32[3,8]{1,0:T(4,128)S(1)}, f32[3,8]{1,0:T(4,128)}, u32[]{:S(2)}) %copy-start) | copy-done | bytes 120
  0.7 0.0 copy-start.1
  0.7 0.7 %copy-done.1 = s32[8]{0:T(128)S(1)} copy-done((s32[8]{0:T(128)S(1)}, s32[8]{0:T(128)}, u32[]{:S(2)}) %copy-start.1) | copy-done | bytes 56
  1.3 0.0 copy-start.2
  1.3 0.7 %copy-done.2 = s32[8]{0:T(128)S(1)} copy-done((s32[8]{0:T(128)S(1)}, s32[8]{0:T(128)}, u32[]{:S(2)}) %copy-start.2) | copy-done | bytes 56
  2.0 0.0 copy-start.3
  2.0 0.7 %copy-done.3 = f32[8]{0:T(128)S(1)} copy-done((f32[8]{0:T(128)S(1)}, f32[8]{0:T(128)}, u32[]{:S(2)}) %copy-start.3) | copy-done | bytes 56
  2.6 39.3 %render.1 = f32[3,32,128]{2,1,0:T(8,128)S(1)} custom-call(f32[32,64,1024]{2,1,0:T(8,128)} %volume.1, s32[8]{0:T(128)S(1)} %copy-done.1, s32[8]{0:T(128)S(1)} %copy-done.2, f32[8]{0:T(128)S(1)} %copy-done.3, f32[3,8]{1,0:T(4,128)S(1)} %copy-done), custom_call_target="tpu_custom_call" | custom-call | tf_op jit(solution)/shard_map/render/pallas_call | solution.py:500
  41.9 0.6 %copy.7 = f32[3,32,128]{2,1,0:T(8,128)} copy(f32[3,32,128]{2,1,0:T(8,128)S(1)} %render.1) | data formatting | bytes 98304
Async XLA Ops:
  0.0 0.7 %copy-start = (f32[3,8]{1,0:T(4,128)S(1)}, f32[3,8]{1,0:T(4,128)}, u32[]{:S(2)}) copy-start(f32[3,8]{1,0:T(4,128)} %color_hbm.1) | copy-start | bytes 292
  0.7 0.7 %copy-start.1 = (s32[8]{0:T(128)S(1)}, s32[8]{0:T(128)}, u32[]{:S(2)}) copy-start(s32[8]{0:T(128)} %place_hbm.1) | copy-start | bytes 100
  1.3 0.7 %copy-start.2 = (s32[8]{0:T(128)S(1)}, s32[8]{0:T(128)}, u32[]{:S(2)}) copy-start(s32[8]{0:T(128)} %index_hbm.1) | copy-start | bytes 100
  2.0 0.7 %copy-start.3 = (f32[8]{0:T(128)S(1)}, f32[8]{0:T(128)}, u32[]{:S(2)}) copy-start(f32[8]{0:T(128)} %extinct_hbm.1) | copy-start | bytes 100

commit v2 on v1

--- a/solution.py
+++ b/solution.py
@@ -91,6 +91,8 @@
     m2_recv,
     out_send,
     out_recv,
+    mate_send,
+    mate_recv,
 ):
     tiles_n, slabs, rows, planes, cols = dims
     ct = cols // LANES
@@ -112,9 +114,6 @@
             ((place_hbm, place), (index_hbm, index), (extinct_hbm, extinct), (color_hbm, color))
         )
     ]
-    for copy in params:
-        copy.start()
-
     def columns(c):
         return pl.ds(pl.multiple_of(c * LANES, LANES), LANES)
 
@@ -127,6 +126,8 @@
 
     for c in range(ct):
         load(c).start()
+    for copy in params:
+        copy.start()
 
     barrier = pltpu.get_barrier_semaphore()
     for j in range(1, slabs):
@@ -144,7 +145,7 @@
         found = jnp.int32(0)
         for s in range(slabs):
             found = jnp.where(place[s] == p, jnp.int32(s), found)
-        slots[p + 1] = lax.rem(me - found + slabs, slabs)
+        slots[p + 1] = found
     zero = jnp.zeros((SUB, LANES), jnp.float32)
     for side in range(2):
         for b in range(blocks):
@@ -169,10 +170,10 @@
             :, side * (planes - 1), columns(owner)
         ]
         if j == 0:
-            return pltpu.make_async_copy(src, face_in.at[0, side], f1_send.at[0, side])
+            return pltpu.make_async_copy(src, face_in.at[me, side], f1_send.at[0, side])
         return pltpu.make_async_remote_copy(
             src_ref=src,
-            dst_ref=face_in.at[j, side],
+            dst_ref=face_in.at[me, side],
             send_sem=f1_send.at[j, side],
             recv_sem=f1_recv.at[j, side],
             device_id={"depth": owner},
@@ -240,6 +241,36 @@
 
     for j in range(1, slabs):
         part_copy(1, j).start()
+
+    pitch = planes + PITCH
+    flat = vol.reshape(ct, (rows + 2) * pitch, LANES)
+
+    def view(p, c, b, shift):
+        return flat[c, pl.ds((b * SUB + 1 + shift) * pitch + p, SUB, stride=pitch), :]
+
+    lane = lax.broadcasted_iota(jnp.int32, (SUB, LANES), 1)
+    sub = lax.broadcasted_iota(jnp.int32, (SUB, LANES), 0)
+
+    def shade_block(b):
+        def step(i, carry):
+            p = i + 1
+            prev, here = carry[:ct], carry[ct:]
+            nxt = tuple(view(p + 1, c, b, 0) for c in range(ct))
+            diffs = col_diffs(here, lane)
+            for c in range(ct):
+                shaded[b, c, p] = shade(
+                    view(p, c, b, 1) - view(p, c, b, -1), nxt[c] - prev[c], diffs[c]
+                )
+            return tuple(here) + nxt
+
+        first = tuple(view(p, c, b, 0) for p in range(2) for c in range(ct))
+        lax.fori_loop(0, planes - 2, step, first, unroll=31)
+
+    def inner(i, _):
+        shade_block(i + 1)
+        return 0
+
+    lax.fori_loop(0, 1, inner, 0)
 
     for j in range(slabs):
         for side in range(2):
@@ -264,43 +295,13 @@
         if j:
             face_second(j).start()
 
-    pitch = planes + PITCH
-    flat = vol.reshape(ct, (rows + 2) * pitch, LANES)
-
-    def view(p, c, b, shift):
-        return flat[c, pl.ds((b * SUB + 1 + shift) * pitch + p, SUB, stride=pitch), :]
-
-    lane = lax.broadcasted_iota(jnp.int32, (SUB, LANES), 1)
-    sub = lax.broadcasted_iota(jnp.int32, (SUB, LANES), 0)
-
-    def shade_block(b):
-        def step(i, carry):
-            p = i + 1
-            prev, here = carry[:ct], carry[ct:]
-            nxt = tuple(view(p + 1, c, b, 0) for c in range(ct))
-            diffs = col_diffs(here, lane)
-            for c in range(ct):
-                shaded[b, c, p] = shade(
-                    view(p, c, b, 1) - view(p, c, b, -1), nxt[c] - prev[c], diffs[c]
-                )
-            return tuple(here) + nxt
-
-        first = tuple(view(p, c, b, 0) for p in range(2) for c in range(ct))
-        lax.fori_loop(0, planes - 2, step, first, unroll=31)
-
-    def inner(i, _):
-        shade_block(i + 1)
-        return 0
-
-    lax.fori_loop(0, 1, inner, 0)
+    lax.fori_loop(1, blocks - 2, inner, 0)
 
     for j in range(1, slabs):
         part_copy(1, j).wait_recv()
     part2[0] = jnp.max(part1[...], axis=0)
     for j in range(1, tiles_n):
         part_copy(2, j).start()
-
-    lax.fori_loop(1, blocks - 2, inner, 0)
 
     def halo_row(side, scale):
         def step(c, _):
@@ -387,66 +388,125 @@
     bounds = [points[k] * unit for k in range(1, knots - 1)]
     odd = jnp.where(sub >= 6, BIG, jnp.where(sub >= 4, bounds[4], jnp.where(sub >= 2, bounds[2], bounds[0])))
 
-    group = 2
-
-    def render_block(b, _):
-        def render_group(g, _):
-            def step(p, carry):
-                out_carry = []
-                for k in range(group):
-                    through, sums = carry[k]
-                    c = g * group + k
-                    dist = view(p, c, b, 0) - low_value
-                    even = jnp.where(dist >= bounds[1], 2, 0)
-                    even = jnp.where(dist >= bounds[3], 4, even)
-                    even = jnp.where(dist >= bounds[5], 6, even)
-                    segment = jnp.where(dist >= lookup(odd, even), even + 1, even)
-                    offset = [lookup(t, segment) for t in offsets]
-                    slope = [lookup(t, segment) for t in slopes]
-                    rest = through * jnp.exp2(offset[0] + slope[0] * dist)
-                    weight = (through - rest) * shaded[b, c, p]
-                    sums = tuple(
-                        sums[i] + weight * (offset[i + 1] + slope[i + 1] * dist) for i in range(3)
-                    )
-                    out_carry.append((rest, sums))
-                return tuple(out_carry)
-
-            begin = tuple((full(1.0), (full(0.0),) * 3) for _ in range(group))
-            done = lax.fori_loop(0, planes, step, begin, unroll=16)
-            for k in range(group):
-                at = columns(g * group + k)
-                for i in range(3):
-                    packed[b, i, :, at] = done[k][1][i]
-                packed[b, 3, :, at] = done[k][0]
+    cores = 2
+    chips = slabs // cores
+    chip = me // cores
+    mate = me + 1 - 2 * lax.rem(me, cores)
+
+    def render(first, b):
+        def step(p, carry):
+            out_carry = []
+            for k in range(cores):
+                through, sums = carry[k]
+                dist = view(p, first + k, b, 0) - low_value
+                even = jnp.where(dist >= bounds[1], 2, 0)
+                even = jnp.where(dist >= bounds[3], 4, even)
+                even = jnp.where(dist >= bounds[5], 6, even)
+                segment = jnp.where(dist >= lookup(odd, even), even + 1, even)
+                offset = [lookup(t, segment) for t in offsets]
+                slope = [lookup(t, segment) for t in slopes]
+                rest = through * jnp.exp2(offset[0] + slope[0] * dist)
+                weight = (through - rest) * shaded[b, first + k, p]
+                sums = tuple(
+                    sums[i] + weight * (offset[i + 1] + slope[i + 1] * dist) for i in range(3)
+                )
+                out_carry.append((rest, sums))
+            return tuple(out_carry)
+
+        begin = tuple((full(1.0), (full(0.0),) * 3) for _ in range(cores))
+        done = lax.fori_loop(0, planes, step, begin, unroll=16)
+        for k in range(cores):
+            for i in range(3):
+                packed[first + k, b, i] = done[k][1][i]
+            packed[first + k, b, 3] = done[k][0]
+
+    def result_copy(owner):
+        return pltpu.make_async_remote_copy(
+            src_ref=packed.at[owner],
+            dst_ref=gathered.at[me],
+            send_sem=out_send.at[owner],
+            recv_sem=out_recv.at[me],
+            device_id={"depth": owner},
+            device_id_type=MESH,
+        )
+
+    def mate_copy(b):
+        return pltpu.make_async_remote_copy(
+            src_ref=packed.at[mate, b],
+            dst_ref=gathered.at[me, b],
+            send_sem=mate_send.at[b],
+            recv_sem=mate_recv.at[b],
+            device_id={"depth": mate},
+            device_id_type=MESH,
+        )
+
+    def away(i, _):
+        first = cores * lax.rem(chip + 2 + (3 * i * i - 5 * i) // 2, chips)
+
+        def block(b, _):
+            render(first, b)
             return 0
 
-        lax.fori_loop(0, ct // group, render_group, 0)
-        for j in range(1, slabs):
-            result_copy(b, j).start()
-        mine = columns(me)
+        lax.fori_loop(0, blocks, block, 0)
+        for k in range(cores):
+            result_copy(first + k).start()
+        return 0
+
+    lax.fori_loop(0, chips - 1, away, 0)
+
+    def home(b, _):
+        render(chip * cores, b)
+        mate_copy(b).start()
         for i in range(4):
-            gathered[b, 0, i] = packed[b, i, :, mine]
+            gathered[me, b, i] = packed[me, b, i]
         return 0
 
-    def result_copy(b, j):
-        peer = depth_peer(j)
-        return pltpu.make_async_remote_copy(
-            src_ref=packed.at[b, :, :, columns(peer)],
-            dst_ref=gathered.at[b, j],
-            send_sem=out_send.at[b, j],
-            recv_sem=out_recv.at[b, j],
-            device_id={"depth": peer},
-            device_id_type=MESH,
-        )
-
-    lax.fori_loop(0, blocks, render_block, 0)
-
-    def arrive(b, _):
-        for j in range(1, slabs):
-            result_copy(b, j).wait_recv()
-        return 0
-
-    lax.fori_loop(0, blocks, arrive, 0)
+    lax.fori_loop(0, blocks, home, 0)
+
+    @pl.when(tile < tiles_n - 1)
+    def _():
+        for c in range(ct):
+            halo(0, c).wait_send()
+
+    @pl.when(tile > 0)
+    def _():
+        for c in range(ct):
+            halo(1, c).wait_send()
+
+    for j in range(1, slabs):
+        for side in range(2):
+            face_first(j, side).wait_send()
+        face_second(j).wait_send()
+        part_copy(1, j).wait_send()
+    for j in range(1, tiles_n):
+        part_copy(2, j).wait_send()
+
+    def away_copy(i):
+        return result_copy(lax.rem(cores * (chip + i // cores) + i % cores, slabs))
+
+    for i in range(cores, slabs):
+        away_copy(i).wait_send()
+    for i in range(cores, slabs):
+        sender = lax.rem(cores * (chip + i // cores) + i % cores, slabs)
+        pltpu.make_async_remote_copy(
+            src_ref=packed.at[sender],
+            dst_ref=gathered.at[sender],
+            send_sem=out_send.at[sender],
+            recv_sem=out_recv.at[sender],
+            device_id={"depth": sender},
+            device_id_type=MESH,
+        ).wait_recv()
+    for b in range(blocks):
+        mate_copy(b).wait_send()
+    for b in range(blocks):
+        pltpu.make_async_remote_copy(
+            src_ref=packed.at[mate, b],
+            dst_ref=gathered.at[mate, b],
+            send_sem=mate_send.at[b],
+            recv_sem=mate_recv.at[b],
+            device_id={"depth": mate},
+            device_id_type=MESH,
+        ).wait_recv()
 
     def composite(b, _):
         rs = pl.ds(pl.multiple_of(b * SUB, SUB), SUB)
@@ -455,38 +515,13 @@
         for p in range(slabs):
             slot = slots[p + 1]
             for i in range(3):
-                sums[i] = sums[i] + through * gathered[b, slot, i]
-            through = through * gathered[b, slot, 3]
+                sums[i] = sums[i] + through * gathered[slot, b, i]
+            through = through * gathered[slot, b, 3]
         for i in range(3):
             out[i, rs, :] = sums[i]
         return 0
 
     lax.fori_loop(0, blocks, composite, 0)
-
-    @pl.when(tile < tiles_n - 1)
-    def _():
-        for c in range(ct):
-            halo(0, c).wait_send()
-
-    @pl.when(tile > 0)
-    def _():
-        for c in range(ct):
-            halo(1, c).wait_send()
-
-    for j in range(1, slabs):
-        for side in range(2):
-            face_first(j, side).wait_send()
-        face_second(j).wait_send()
-        part_copy(1, j).wait_send()
-    for j in range(1, tiles_n):
-        part_copy(2, j).wait_send()
-
-    def drain(b, _):
-        for j in range(1, slabs):
-            result_copy(b, j).wait_send()
-        return 0
-
-    lax.fori_loop(0, blocks, drain, 0)
 
 
 def solution(mesh):
@@ -500,7 +535,7 @@
         return pl.pallas_call(
             functools.partial(kernel, dims),
             out_shape=jax.ShapeDtypeStruct((3, rows, cols // slabs), f32),
-            in_specs=[pl.BlockSpec(memory_space=pl.ANY)] * 5,
+            in_specs=[pl.BlockSpec(memory_space=pltpu.HBM)] * 5,
             out_specs=pl.BlockSpec(memory_space=pltpu.VMEM),
             scratch_shapes=[
                 pltpu.VMEM((ct, rows + 2, planes + PITCH, LANES), f32),
@@ -510,8 +545,8 @@
                 pltpu.VMEM((slabs, 2, rows, LANES), f32),
                 pltpu.VMEM((slabs, 2, LANES), f32),
                 pltpu.VMEM((tiles_n, 2, LANES), f32),
-                pltpu.VMEM((blocks, 4, SUB, cols), f32),
-                pltpu.VMEM((blocks, slabs, 4, SUB, LANES), f32),
+                pltpu.VMEM((slabs, blocks, 4, SUB, LANES), f32),
+                pltpu.VMEM((slabs, blocks, 4, SUB, LANES), f32),
                 pltpu.SMEM(slab_place.shape, jnp.int32),
                 pltpu.SMEM(control_index.shape, jnp.int32),
                 pltpu.SMEM(control_extinction.shape, f32),
@@ -529,11 +564,13 @@
                 dma((slabs,)),
                 dma((tiles_n,)),
                 dma((tiles_n,)),
-                dma((blocks, slabs)),
-                dma((blocks, slabs)),
+                dma((slabs,)),
+                dma((slabs,)),
+                dma((blocks,)),
+                dma((blocks,)),
             ],
             compiler_params=pltpu.CompilerParams(
-                collective_id=0, has_side_effects=True, vmem_limit_bytes=48 << 20
+                collective_id=0, has_side_effects=True, vmem_limit_bytes=63 << 20
             ),
             name="render",
         )(volume, slab_place, control_index, control_extinction, control_color)

time: 42.7 us -> 36.5 us (0.85)
  Pallas kernels: 39.3 us -> 34.9 us
  local copies, waits for them, and re-layouts: 3.27 us -> 1.42 us
    pallas_call x1, Pallas kernels: 39.3 us -> 34.9 us  [body(): pl.pallas_call(functools.partial(kernel, dims), out_shape=jax.ShapeDtypeS...]
    unnamed x9 -> x1, local copies, waits for them, and re-layouts: 3.27 us -> 1.42 us
where the time goes in v2:
time: 36.5 us; the launch traced here: 36.3 us
  Pallas kernels  34.9 us (96%)
  local copies, waits for them, and re-layouts  1.42 us (4%)
    pallas_call x1, Pallas kernels, body(): pl.pallas_call(functools.partial(kernel, dims), out_shape=jax.ShapeDtypeS...  34.9 us
    unnamed x1, local copies, waits for them, and re-layouts  1.42 us

profile of v2, /device:TPU:1, one launch (start us, length us, event | category | flops | bytes accessed | tf_op | source)
XLA Modules:
  0.0 36.3 jit_solution(11005790188288489555)
XLA Ops:
  0.0 34.9 %render.1 = f32[3,32,128]{2,1,0:T(8,128)} custom-call(f32[32,64,1024]{2,1,0:T(8,128)} %volume.1, s32[8]{0:T(128)} %place_hbm.1, s32[8]{0:T(128)} %index_hbm.1, f32[8]{0:T(128)} %extinct_hbm.1, f32[3,8]{1,0:T(4,128)} %color_hbm.1), custom_call_target="tpu_custom_call" | custom-call | tf_op jit(solution)/shard_map/render/pallas_call | solution.py:535
  34.9 1.4 %copy.7 = f32[3,32,128]{2,1,0:T(8,128)} copy(f32[3,32,128]{2,1,0:T(8,128)} %render.1) | data formatting | bytes 98304

commit v3 on v1

--- a/solution.py
+++ b/solution.py
@@ -42,17 +42,16 @@
     return BASE + jnp.abs(facing) * lax.rsqrt(norm)
 
 
-def col_diffs(tiles, lane):
-    right = [pltpu.roll(x, 1, 1) for x in tiles]
-    left = [pltpu.roll(x, LANES - 1, 1) for x in tiles]
-    zero = jnp.zeros((SUB, LANES), jnp.float32)
-    last = len(tiles) - 1
-    out = []
-    for c in range(len(tiles)):
-        prev = jnp.where(lane == 0, right[c - 1] if c else zero, right[c])
-        nxt = jnp.where(lane == LANES - 1, left[c + 1] if c < last else zero, left[c])
-        out.append(nxt - prev)
-    return out
+def col_diffs(tiles, before, after, lane):
+    right = [None if x is None else pltpu.roll(x, 1, 1) for x in (before, *tiles)]
+    left = [None if x is None else pltpu.roll(x, LANES - 1, 1) for x in (*tiles, after)]
+    right = [jnp.zeros_like(tiles[0]) if x is None else x for x in right]
+    left = [jnp.zeros_like(tiles[0]) if x is None else x for x in left]
+    return [
+        jnp.where(lane == LANES - 1, left[k + 1], left[k])
+        - jnp.where(lane == 0, right[k], right[k + 1])
+        for k in range(len(tiles))
+    ]
 
 
 def kernel(
@@ -112,9 +111,6 @@
             ((place_hbm, place), (index_hbm, index), (extinct_hbm, extinct), (color_hbm, color))
         )
     ]
-    for copy in params:
-        copy.start()
-
     def columns(c):
         return pl.ds(pl.multiple_of(c * LANES, LANES), LANES)
 
@@ -127,6 +123,8 @@
 
     for c in range(ct):
         load(c).start()
+    for copy in params:
+        copy.start()
 
     barrier = pltpu.get_barrier_semaphore()
     for j in range(1, slabs):
@@ -144,7 +142,7 @@
         found = jnp.int32(0)
         for s in range(slabs):
             found = jnp.where(place[s] == p, jnp.int32(s), found)
-        slots[p + 1] = lax.rem(me - found + slabs, slabs)
+        slots[p + 1] = found
     zero = jnp.zeros((SUB, LANES), jnp.float32)
     for side in range(2):
         for b in range(blocks):
@@ -169,10 +167,10 @@
             :, side * (planes - 1), columns(owner)
         ]
         if j == 0:
-            return pltpu.make_async_copy(src, face_in.at[0, side], f1_send.at[0, side])
+            return pltpu.make_async_copy(src, face_in.at[me, side], f1_send.at[0, side])
         return pltpu.make_async_remote_copy(
             src_ref=src,
-            dst_ref=face_in.at[j, side],
+            dst_ref=face_in.at[me, side],
             send_sem=f1_send.at[j, side],
             recv_sem=f1_recv.at[j, side],
             device_id={"depth": owner},
@@ -202,6 +200,43 @@
     def _():
         for c in range(ct):
             halo(1, c).start()
+
+    pitch = planes + PITCH
+    flat = vol.reshape(ct, (rows + 2) * pitch, LANES)
+
+    def view(p, c, b, shift):
+        return flat[c, pl.ds((b * SUB + 1 + shift) * pitch + p, SUB, stride=pitch), :]
+
+    lane = lax.broadcasted_iota(jnp.int32, (SUB, LANES), 1)
+    sub = lax.broadcasted_iota(jnp.int32, (SUB, LANES), 0)
+
+    run = 2
+
+    def shade_run(first, b):
+        tiles = range(first, first + run)
+
+        def step(i, carry):
+            p = i + 1
+            prev, here = carry[:run], carry[run:]
+            nxt = tuple(view(p + 1, c, b, 0) for c in tiles)
+            before = view(p, first - 1, b, 0) if first else None
+            after = view(p, first + run, b, 0) if first + run < ct else None
+            diffs = col_diffs(here, before, after, lane)
+            for k, c in enumerate(tiles):
+                shaded[b, c, p] = shade(
+                    view(p, c, b, 1) - view(p, c, b, -1), nxt[k] - prev[k], diffs[k]
+                )
+            return tuple(here) + nxt
+
+        first_two = tuple(view(p, c, b, 0) for p in range(2) for c in tiles)
+        lax.fori_loop(0, planes - 2, step, first_two, unroll=31)
+
+    def shade_inner(first):
+        def block(b, _):
+            shade_run(first, b)
+            return 0
+
+        lax.fori_loop(1, blocks - 1, block, 0)
 
     pieces = planes // SUB
 
@@ -222,7 +257,11 @@
         return lax.fori_loop(0, rows, step, carry, unroll=4)
 
     start = (tuple([full(-BIG)] * pieces), tuple([full(BIG)] * pieces))
-    high, low = lax.fori_loop(0, ct, extremes_block, start)
+    extremes = lax.fori_loop(0, run + 1, extremes_block, start)
+    shade_inner(0)
+    extremes = lax.fori_loop(run + 1, 2 * run + 1, extremes_block, extremes)
+    shade_inner(run)
+    high, low = lax.fori_loop(2 * run + 1, ct, extremes_block, extremes)
     part1[0, 0:1, :] = jnp.max(functools.reduce(jnp.maximum, high), axis=0, keepdims=True)
     part1[0, 1:2, :] = -jnp.min(functools.reduce(jnp.minimum, low), axis=0, keepdims=True)
 
@@ -240,6 +279,8 @@
 
     for j in range(1, slabs):
         part_copy(1, j).start()
+
+    shade_inner(2 * run)
 
     for j in range(slabs):
         for side in range(2):
@@ -264,43 +305,13 @@
         if j:
             face_second(j).start()
 
-    pitch = planes + PITCH
-    flat = vol.reshape(ct, (rows + 2) * pitch, LANES)
-
-    def view(p, c, b, shift):
-        return flat[c, pl.ds((b * SUB + 1 + shift) * pitch + p, SUB, stride=pitch), :]
-
-    lane = lax.broadcasted_iota(jnp.int32, (SUB, LANES), 1)
-    sub = lax.broadcasted_iota(jnp.int32, (SUB, LANES), 0)
-
-    def shade_block(b):
-        def step(i, carry):
-            p = i + 1
-            prev, here = carry[:ct], carry[ct:]
-            nxt = tuple(view(p + 1, c, b, 0) for c in range(ct))
-            diffs = col_diffs(here, lane)
-            for c in range(ct):
-                shaded[b, c, p] = shade(
-                    view(p, c, b, 1) - view(p, c, b, -1), nxt[c] - prev[c], diffs[c]
-                )
-            return tuple(here) + nxt
-
-        first = tuple(view(p, c, b, 0) for p in range(2) for c in range(ct))
-        lax.fori_loop(0, planes - 2, step, first, unroll=31)
-
-    def inner(i, _):
-        shade_block(i + 1)
-        return 0
-
-    lax.fori_loop(0, 1, inner, 0)
+    shade_inner(3 * run)
 
     for j in range(1, slabs):
         part_copy(1, j).wait_recv()
     part2[0] = jnp.max(part1[...], axis=0)
     for j in range(1, tiles_n):
         part_copy(2, j).start()
-
-    lax.fori_loop(1, blocks - 2, inner, 0)
 
     def halo_row(side, scale):
         def step(c, _):
@@ -330,7 +341,8 @@
         halo_row(1, False)
 
     def outer(i, _):
-        shade_block(i * (blocks - 1))
+        for first in range(0, ct, run):
+            shade_run(first, i * (blocks - 1))
         return 0
 
     lax.fori_loop(0, 2, outer, 0)
@@ -342,7 +354,7 @@
         rs = pl.ds(pl.multiple_of(b * SUB, SUB), SUB)
         for side in range(2):
             p = side * (planes - 1)
-            diffs = col_diffs([view(p, c, b, 0) for c in range(ct)], lane)
+            diffs = col_diffs([view(p, c, b, 0) for c in range(ct)], None, None, lane)
             for c in range(ct):
                 other = face[c, side, rs, :]
                 if side == 0:
@@ -387,16 +399,20 @@
     bounds = [points[k] * unit for k in range(1, knots - 1)]
     odd = jnp.where(sub >= 6, BIG, jnp.where(sub >= 4, bounds[4], jnp.where(sub >= 2, bounds[2], bounds[0])))
 
-    group = 2
-
-    def render_block(b, _):
-        def render_group(g, _):
+    cores = 2
+    chips = slabs // cores
+    chip = me // cores
+    mate = me + 1 - 2 * lax.rem(me, cores)
+    pair = 2
+
+    def render(owner, result):
+        def rows_pair(i, _):
             def step(p, carry):
                 out_carry = []
-                for k in range(group):
+                for k in range(pair):
+                    b = i * pair + k
                     through, sums = carry[k]
-                    c = g * group + k
-                    dist = view(p, c, b, 0) - low_value
+                    dist = view(p, owner, b, 0) - low_value
                     even = jnp.where(dist >= bounds[1], 2, 0)
                     even = jnp.where(dist >= bounds[3], 4, even)
                     even = jnp.where(dist >= bounds[5], 6, even)
@@ -404,49 +420,68 @@
                     offset = [lookup(t, segment) for t in offsets]
                     slope = [lookup(t, segment) for t in slopes]
                     rest = through * jnp.exp2(offset[0] + slope[0] * dist)
-                    weight = (through - rest) * shaded[b, c, p]
+                    weight = (through - rest) * shaded[b, owner, p]
                     sums = tuple(
-                        sums[i] + weight * (offset[i + 1] + slope[i + 1] * dist) for i in range(3)
+                        sums[n] + weight * (offset[n + 1] + slope[n + 1] * dist)
+                        for n in range(3)
                     )
                     out_carry.append((rest, sums))
                 return tuple(out_carry)
 
-            begin = tuple((full(1.0), (full(0.0),) * 3) for _ in range(group))
-            done = lax.fori_loop(0, planes, step, begin, unroll=16)
-            for k in range(group):
-                at = columns(g * group + k)
-                for i in range(3):
-                    packed[b, i, :, at] = done[k][1][i]
-                packed[b, 3, :, at] = done[k][0]
+            begin = tuple((full(1.0), (full(0.0),) * 3) for _ in range(pair))
+            done = lax.fori_loop(0, planes, step, begin, unroll=32)
+            for k in range(pair):
+                for n in range(3):
+                    result[owner, i * pair + k, n] = done[k][1][n]
+                result[owner, i * pair + k, 3] = done[k][0]
             return 0
 
-        lax.fori_loop(0, ct // group, render_group, 0)
-        for j in range(1, slabs):
-            result_copy(b, j).start()
-        mine = columns(me)
-        for i in range(4):
-            gathered[b, 0, i] = packed[b, i, :, mine]
+        lax.fori_loop(0, blocks // pair, rows_pair, 0)
+
+    def result_copy(owner, sender):
+        return pltpu.make_async_remote_copy(
+            src_ref=packed.at[owner],
+            dst_ref=gathered.at[sender],
+            send_sem=out_send.at[owner],
+            recv_sem=out_recv.at[sender],
+            device_id={"depth": owner},
+            device_id_type=MESH,
+        )
+
+    def away(i, _):
+        n = i // cores
+        owner = cores * lax.rem(chip + 2 + (3 * n * n - 5 * n) // 2, chips) + i % cores
+        render(owner, packed)
+        result_copy(owner, me).start()
         return 0
 
-    def result_copy(b, j):
-        peer = depth_peer(j)
-        return pltpu.make_async_remote_copy(
-            src_ref=packed.at[b, :, :, columns(peer)],
-            dst_ref=gathered.at[b, j],
-            send_sem=out_send.at[b, j],
-            recv_sem=out_recv.at[b, j],
-            device_id={"depth": peer},
-            device_id_type=MESH,
-        )
-
-    lax.fori_loop(0, blocks, render_block, 0)
-
-    def arrive(b, _):
-        for j in range(1, slabs):
-            result_copy(b, j).wait_recv()
-        return 0
-
-    lax.fori_loop(0, blocks, arrive, 0)
+    lax.fori_loop(0, slabs - cores, away, 0)
+    render(mate, packed)
+    result_copy(mate, me).start()
+    render(me, gathered)
+
+    @pl.when(tile < tiles_n - 1)
+    def _():
+        for c in range(ct):
+            halo(0, c).wait_send()
+
+    @pl.when(tile > 0)
+    def _():
+        for c in range(ct):
+            halo(1, c).wait_send()
+
+    for j in range(1, slabs):
+        for side in range(2):
+            face_first(j, side).wait_send()
+        face_second(j).wait_send()
+        part_copy(1, j).wait_send()
+    for j in range(1, tiles_n):
+        part_copy(2, j).wait_send()
+
+    for j in range(1, slabs):
+        result_copy(depth_peer(j), me).wait_send()
+    for j in range(1, slabs):
+        result_copy(depth_peer(j), depth_peer(j)).wait_recv()
 
     def composite(b, _):
         rs = pl.ds(pl.multiple_of(b * SUB, SUB), SUB)
@@ -455,38 +490,13 @@
         for p in range(slabs):
             slot = slots[p + 1]
             for i in range(3):
-                sums[i] = sums[i] + through * gathered[b, slot, i]
-            through = through * gathered[b, slot, 3]
+                sums[i] = sums[i] + through * gathered[slot, b, i]
+            through = through * gathered[slot, b, 3]
         for i in range(3):
             out[i, rs, :] = sums[i]
         return 0
 
     lax.fori_loop(0, blocks, composite, 0)
-
-    @pl.when(tile < tiles_n - 1)
-    def _():
-        for c in range(ct):
-            halo(0, c).wait_send()
-
-    @pl.when(tile > 0)
-    def _():
-        for c in range(ct):
-            halo(1, c).wait_send()
-
-    for j in range(1, slabs):
-        for side in range(2):
-            face_first(j, side).wait_send()
-        face_second(j).wait_send()
-        part_copy(1, j).wait_send()
-    for j in range(1, tiles_n):
-        part_copy(2, j).wait_send()
-
-    def drain(b, _):
-        for j in range(1, slabs):
-            result_copy(b, j).wait_send()
-        return 0
-
-    lax.fori_loop(0, blocks, drain, 0)
 
 
 def solution(mesh):
@@ -500,7 +510,7 @@
         return pl.pallas_call(
             functools.partial(kernel, dims),
             out_shape=jax.ShapeDtypeStruct((3, rows, cols // slabs), f32),
-            in_specs=[pl.BlockSpec(memory_space=pl.ANY)] * 5,
+            in_specs=[pl.BlockSpec(memory_space=pltpu.HBM)] * 5,
             out_specs=pl.BlockSpec(memory_space=pltpu.VMEM),
             scratch_shapes=[
                 pltpu.VMEM((ct, rows + 2, planes + PITCH, LANES), f32),
@@ -510,8 +520,8 @@
                 pltpu.VMEM((slabs, 2, rows, LANES), f32),
                 pltpu.VMEM((slabs, 2, LANES), f32),
                 pltpu.VMEM((tiles_n, 2, LANES), f32),
-                pltpu.VMEM((blocks, 4, SUB, cols), f32),
-                pltpu.VMEM((blocks, slabs, 4, SUB, LANES), f32),
+                pltpu.VMEM((slabs, blocks, 4, SUB, LANES), f32),
+                pltpu.VMEM((slabs, blocks, 4, SUB, LANES), f32),
                 pltpu.SMEM(slab_place.shape, jnp.int32),
                 pltpu.SMEM(control_index.shape, jnp.int32),
                 pltpu.SMEM(control_extinction.shape, f32),
@@ -529,14 +539,20 @@
                 dma((slabs,)),
                 dma((tiles_n,)),
                 dma((tiles_n,)),
-                dma((blocks, slabs)),
-                dma((blocks, slabs)),
+                dma((slabs,)),
+                dma((slabs,)),
             ],
             compiler_params=pltpu.CompilerParams(
                 collective_id=0, has_side_effects=True, vmem_limit_bytes=48 << 20
             ),
             name="render",
-        )(volume, slab_place, control_index, control_extinction, control_color)
+        )(
+            volume,
+            *(
+                pltpu.with_memory_space_constraint(x, pltpu.HBM)
+                for x in (slab_place, control_index, control_extinction, control_color)
+            ),
+        )
 
     placed = (P("tile", "depth", None), P(), P(), P(), P())
     return jax.shard_map(

time: 42.7 us -> 34.7 us (0.81)
  Pallas kernels: 39.3 us -> 34 us
  local copies, waits for them, and re-layouts: 3.27 us -> 0.62 us
    pallas_call x1, Pallas kernels: 39.3 us -> 34 us  [body(): pl.pallas_call(functools.partial(kernel, dims), out_shape=jax.ShapeDtypeS...]
    unnamed x9 -> x1, local copies, waits for them, and re-layouts: 3.27 us -> 0.62 us
where the time goes in v3:
time: 34.7 us; the launch traced here: 34.6 us
  Pallas kernels  34 us (98%)
  local copies, waits for them, and re-layouts  0.62 us (2%)
    pallas_call x1, Pallas kernels, body(): pl.pallas_call(functools.partial(kernel, dims), out_shape=jax.ShapeDtypeS...  34 us

profile of v3, /device:TPU:1, one launch (start us, length us, event | category | flops | bytes accessed | tf_op | source)
XLA Modules:
  0.0 34.6 jit_solution(9120458002353087913)
XLA Ops:
  0.0 34.0 %render.1 = f32[3,32,128]{2,1,0:T(8,128)S(1)} custom-call(f32[32,64,1024]{2,1,0:T(8,128)} %volume.1, s32[8]{0:T(128)} %place_hbm.1, s32[8]{0:T(128)} %index_hbm.1, f32[8]{0:T(128)} %extinct_hbm.1, f32[3,8]{1,0:T(4,128)} %color_hbm.1), custom_call_target="tpu_custom_call" | custom-call | tf_op jit(solution)/shard_map/render/pallas_call | solution.py:510
  34.0 0.6 %copy.7 = f32[3,32,128]{2,1,0:T(8,128)} copy(f32[3,32,128]{2,1,0:T(8,128)S(1)} %render.1) | data formatting | bytes 98304

commit v4 on v3

--- a/solution.py
+++ b/solution.py
@@ -12,7 +12,6 @@
 TABLE = 256
 LANES = 128
 SUB = 8
-PITCH = 8
 KA, KB, KC = 0.48 / 0.64, 0.6 / 0.64, 0.7 * 0.64
 BASE = 0.3 / KC
 LOG2E = float(np.log2(np.e))
@@ -43,15 +42,13 @@
 
 
 def col_diffs(tiles, before, after, lane):
-    right = [None if x is None else pltpu.roll(x, 1, 1) for x in (before, *tiles)]
-    left = [None if x is None else pltpu.roll(x, LANES - 1, 1) for x in (*tiles, after)]
-    right = [jnp.zeros_like(tiles[0]) if x is None else x for x in right]
-    left = [jnp.zeros_like(tiles[0]) if x is None else x for x in left]
-    return [
-        jnp.where(lane == LANES - 1, left[k + 1], left[k])
-        - jnp.where(lane == 0, right[k], right[k + 1])
-        for k in range(len(tiles))
-    ]
+    wide = (before, *tiles, after)
+    out = []
+    for k in range(1, len(wide) - 1):
+        nxt = pltpu.roll(jnp.where(lane == 0, wide[k + 1], wide[k]), LANES - 1, 1)
+        prev = pltpu.roll(jnp.where(lane == LANES - 1, wide[k - 1], wide[k]), 1, 1)
+        out.append(nxt - prev)
+    return out
 
 
 def kernel(
@@ -62,6 +59,7 @@
     extinct_hbm,
     color_hbm,
     out,
+    raw,
     vol,
     shaded,
     face_in,
@@ -117,7 +115,7 @@
     def load(c):
         return pltpu.make_async_copy(
             volume.at[:, :, columns(c)],
-            vol.at[c, pl.ds(1, rows), pl.ds(0, planes), :],
+            raw.at[c],
             load_sem.at[c],
         )
 
@@ -154,7 +152,7 @@
         row = rows - 1 if side == 0 else 0
         return pltpu.make_async_remote_copy(
             src_ref=volume.at[row, :, columns(c)],
-            dst_ref=vol.at[c, rows + 1 if side else 0, pl.ds(0, planes), :],
+            dst_ref=vol.at[c, pl.ds(side, planes), 0 if side else SUB - 1, :],
             send_sem=halo_send.at[side, c],
             recv_sem=halo_recv.at[side, c],
             device_id={"tile": above if side else below},
@@ -201,26 +199,32 @@
         for c in range(ct):
             halo(1, c).start()
 
-    pitch = planes + PITCH
-    flat = vol.reshape(ct, (rows + 2) * pitch, LANES)
+    pitch = rows + SUB
+    flat = vol.reshape(ct, (planes + 1) * pitch, LANES)
 
     def view(p, c, b, shift):
-        return flat[c, pl.ds((b * SUB + 1 + shift) * pitch + p, SUB, stride=pitch), :]
+        if shift == 0:
+            return flat[c, pl.ds(pl.multiple_of(p * pitch + (b + 1) * SUB, SUB), SUB), :]
+        window = flat.at[c, pl.ds(pl.multiple_of(p * pitch + b * SUB, SUB), 3 * SUB), :]
+        return window[SUB + shift : 2 * SUB + shift, :]
+
+    def planes_of(q, row):
+        return pl.ds(q * SUB * pitch + row, SUB, stride=pitch)
 
     lane = lax.broadcasted_iota(jnp.int32, (SUB, LANES), 1)
     sub = lax.broadcasted_iota(jnp.int32, (SUB, LANES), 0)
 
     run = 2
 
-    def shade_run(first, b):
-        tiles = range(first, first + run)
+    def shade_run(first, count, b, unroll):
+        tiles = range(first, first + count)
 
         def step(i, carry):
             p = i + 1
-            prev, here = carry[:run], carry[run:]
+            prev, here = carry[:count], carry[count:]
             nxt = tuple(view(p + 1, c, b, 0) for c in tiles)
-            before = view(p, first - 1, b, 0) if first else None
-            after = view(p, first + run, b, 0) if first + run < ct else None
+            before = view(p, first - 1, b, 0) if first else zero
+            after = view(p, first + count, b, 0) if first + count < ct else zero
             diffs = col_diffs(here, before, after, lane)
             for k, c in enumerate(tiles):
                 shaded[b, c, p] = shade(
@@ -229,11 +233,11 @@
             return tuple(here) + nxt
 
         first_two = tuple(view(p, c, b, 0) for p in range(2) for c in tiles)
-        lax.fori_loop(0, planes - 2, step, first_two, unroll=31)
+        lax.fori_loop(0, planes - 2, step, first_two, unroll=unroll)
 
     def shade_inner(first):
         def block(b, _):
-            shade_run(first, b)
+            shade_run(first, run, b, 31)
             return 0
 
         lax.fori_loop(1, blocks - 1, block, 0)
@@ -247,9 +251,8 @@
             high, low = carry
             new_high, new_low = [], []
             for q in range(pieces):
-                at = vol.at[c, r + 1, pl.ds(q * SUB, SUB), :]
-                half = at[...] * 0.5
-                at[...] = half
+                half = raw[c, r, pl.ds(q * SUB, SUB), :] * 0.5
+                flat[c, planes_of(q, SUB + r), :] = half
                 new_high.append(jnp.maximum(high[q], half))
                 new_low.append(jnp.minimum(low[q], half))
             return tuple(new_high), tuple(new_low)
@@ -318,8 +321,8 @@
             if scale:
                 halo(side, c).wait_recv()
             for q in range(pieces):
-                at = vol.at[c, rows + 1 if side else 0, pl.ds(q * SUB, SUB), :]
-                at[...] = at[...] * 0.5 if scale else zero
+                at = planes_of(q, pitch if side else SUB - 1)
+                flat[c, at, :] = flat[c, at, :] * 0.5 if scale else zero
             return 0
 
         lax.fori_loop(0, ct, step, 0)
@@ -341,8 +344,7 @@
         halo_row(1, False)
 
     def outer(i, _):
-        for first in range(0, ct, run):
-            shade_run(first, i * (blocks - 1))
+        shade_run(0, ct, i * (blocks - 1), 31)
         return 0
 
     lax.fori_loop(0, 2, outer, 0)
@@ -354,7 +356,7 @@
         rs = pl.ds(pl.multiple_of(b * SUB, SUB), SUB)
         for side in range(2):
             p = side * (planes - 1)
-            diffs = col_diffs([view(p, c, b, 0) for c in range(ct)], None, None, lane)
+            diffs = col_diffs([view(p, c, b, 0) for c in range(ct)], zero, zero, lane)
             for c in range(ct):
                 other = face[c, side, rs, :]
                 if side == 0:
@@ -513,7 +515,8 @@
             in_specs=[pl.BlockSpec(memory_space=pltpu.HBM)] * 5,
             out_specs=pl.BlockSpec(memory_space=pltpu.VMEM),
             scratch_shapes=[
-                pltpu.VMEM((ct, rows + 2, planes + PITCH, LANES), f32),
+                pltpu.VMEM((ct, rows, planes, LANES), f32),
+                pltpu.VMEM((ct, planes + 1, rows + SUB, LANES), f32),
                 pltpu.VMEM((blocks, ct, planes, SUB, LANES), f32),
                 pltpu.VMEM((slabs + 1, 2, rows, LANES), f32),
                 pltpu.VMEM((slabs, 2, rows, LANES), f32),

time: 34.7 us -> 33.8 us (0.974)
  Pallas kernels: 34 us -> 33.1 us
    pallas_call x1, Pallas kernels: 34 us -> 33.1 us  [body(): pl.pallas_call(functools.partial(kernel, dims), out_shape=jax.ShapeDtypeS...]
where the time goes in v4:
time: 33.8 us; the launch traced here: 33.7 us
  Pallas kernels  33.1 us (98%)
  local copies, waits for them, and re-layouts  0.62 us (2%)
    pallas_call x1, Pallas kernels, body(): pl.pallas_call(functools.partial(kernel, dims), out_shape=jax.ShapeDtypeS...  33.1 us

profile of v4, /device:TPU:1, one launch (start us, length us, event | category | flops | bytes accessed | tf_op | source)
XLA Modules:
  0.0 33.7 jit_solution(5666589692516192422)
XLA Ops:
  0.0 33.1 %render.1 = f32[3,32,128]{2,1,0:T(8,128)S(1)} custom-call(f32[32,64,1024]{2,1,0:T(8,128)} %volume.1, s32[8]{0:T(128)} %place_hbm.1, s32[8]{0:T(128)} %index_hbm.1, f32[8]{0:T(128)} %extinct_hbm.1, f32[3,8]{1,0:T(4,128)} %color_hbm.1), custom_call_target="tpu_custom_call" | custom-call | tf_op jit(solution)/shard_map/render/pallas_call | solution.py:512
  33.1 0.6 %copy.7 = f32[3,32,128]{2,1,0:T(8,128)} copy(f32[3,32,128]{2,1,0:T(8,128)S(1)} %render.1) | data formatting | bytes 98304

commit v5 on v4

--- a/solution.py
+++ b/solution.py
@@ -78,6 +78,7 @@
     load_sem,
     halo_send,
     halo_recv,
+    f1_own,
     f1_send,
     f1_recv,
     f2_send,
@@ -103,6 +104,9 @@
     def tile_peer(j):
         return lax.rem(tile + j, tiles_n)
 
+    def wait_all(like, sem):
+        pltpu.make_async_copy(like, like, sem).wait()
+
     params = [
         pltpu.make_async_copy(src, dst, param_sem.at[i])
         for i, (src, dst) in enumerate(
@@ -153,8 +157,8 @@
         return pltpu.make_async_remote_copy(
             src_ref=volume.at[row, :, columns(c)],
             dst_ref=vol.at[c, pl.ds(side, planes), 0 if side else SUB - 1, :],
-            send_sem=halo_send.at[side, c],
-            recv_sem=halo_recv.at[side, c],
+            send_sem=halo_send.at[side],
+            recv_sem=halo_recv.at[side],
             device_id={"tile": above if side else below},
             device_id_type=MESH,
         )
@@ -165,12 +169,12 @@
             :, side * (planes - 1), columns(owner)
         ]
         if j == 0:
-            return pltpu.make_async_copy(src, face_in.at[me, side], f1_send.at[0, side])
+            return pltpu.make_async_copy(src, face_in.at[me, side], f1_own)
         return pltpu.make_async_remote_copy(
             src_ref=src,
             dst_ref=face_in.at[me, side],
-            send_sem=f1_send.at[j, side],
-            recv_sem=f1_recv.at[j, side],
+            send_sem=f1_send,
+            recv_sem=f1_recv,
             device_id={"depth": owner},
             device_id_type=MESH,
         )
@@ -179,8 +183,8 @@
         return pltpu.make_async_remote_copy(
             src_ref=face_out.at[j],
             dst_ref=face.at[me],
-            send_sem=f2_send.at[j],
-            recv_sem=f2_recv.at[j],
+            send_sem=f2_send,
+            recv_sem=f2_recv,
             device_id={"depth": depth_peer(j)},
             device_id_type=MESH,
         )
@@ -237,7 +241,7 @@
 
     def shade_inner(first):
         def block(b, _):
-            shade_run(first, run, b, 31)
+            shade_run(first, run, b, planes - 2)
             return 0
 
         lax.fori_loop(1, blocks - 1, block, 0)
@@ -274,8 +278,8 @@
         return pltpu.make_async_remote_copy(
             src_ref=buf.at[0],
             dst_ref=buf.at[j],
-            send_sem=send.at[j],
-            recv_sem=recv.at[j],
+            send_sem=send,
+            recv_sem=recv,
             device_id=peer,
             device_id_type=MESH,
         )
@@ -285,12 +289,9 @@
 
     shade_inner(2 * run)
 
-    for j in range(slabs):
-        for side in range(2):
-            if j == 0:
-                face_first(j, side).wait()
-            else:
-                face_first(j, side).wait_recv()
+    others = slabs - 1
+    wait_all(face_in.at[0], f1_own)
+    wait_all(face_in.at[pl.ds(0, others)], f1_recv)
     for j in range(slabs):
         at = place[depth_peer(j)]
         front = slots[at]
@@ -310,16 +311,16 @@
 
     shade_inner(3 * run)
 
-    for j in range(1, slabs):
-        part_copy(1, j).wait_recv()
+    wait_all(part1.at[pl.ds(1, others)], m1_recv)
     part2[0] = jnp.max(part1[...], axis=0)
     for j in range(1, tiles_n):
         part_copy(2, j).start()
 
     def halo_row(side, scale):
+        if scale:
+            wait_all(vol.at[:, pl.ds(side, planes), 0 if side else SUB - 1, :], halo_recv.at[side])
+
         def step(c, _):
-            if scale:
-                halo(side, c).wait_recv()
             for q in range(pieces):
                 at = planes_of(q, pitch if side else SUB - 1)
                 flat[c, at, :] = flat[c, at, :] * 0.5 if scale else zero
@@ -349,8 +350,7 @@
 
     lax.fori_loop(0, 2, outer, 0)
 
-    for j in range(1, slabs):
-        face_second(j).wait_recv()
+    wait_all(face.at[pl.ds(0, others)], f2_recv)
 
     def edge_planes(b, _):
         rs = pl.ds(pl.multiple_of(b * SUB, SUB), SUB)
@@ -390,8 +390,7 @@
         offsets.append((begin - slope * lower) * scale)
         slopes.append(slope * scale)
 
-    for j in range(1, tiles_n):
-        part_copy(2, j).wait_recv()
+    wait_all(part2.at[pl.ds(1, tiles_n - 1)], m2_recv)
     extremes = jnp.max(jnp.max(part2[...], axis=0), axis=1, keepdims=True)
     extremes = jnp.broadcast_to(extremes, (2, LANES))
     low_value = jnp.broadcast_to(-extremes[1:2, :], (SUB, LANES))
@@ -440,12 +439,12 @@
 
         lax.fori_loop(0, blocks // pair, rows_pair, 0)
 
-    def result_copy(owner, sender):
+    def result_copy(owner):
         return pltpu.make_async_remote_copy(
             src_ref=packed.at[owner],
-            dst_ref=gathered.at[sender],
-            send_sem=out_send.at[owner],
-            recv_sem=out_recv.at[sender],
+            dst_ref=gathered.at[me],
+            send_sem=out_send,
+            recv_sem=out_recv,
             device_id={"depth": owner},
             device_id_type=MESH,
         )
@@ -454,36 +453,29 @@
         n = i // cores
         owner = cores * lax.rem(chip + 2 + (3 * n * n - 5 * n) // 2, chips) + i % cores
         render(owner, packed)
-        result_copy(owner, me).start()
+        result_copy(owner).start()
         return 0
 
     lax.fori_loop(0, slabs - cores, away, 0)
     render(mate, packed)
-    result_copy(mate, me).start()
+    result_copy(mate).start()
     render(me, gathered)
 
     @pl.when(tile < tiles_n - 1)
     def _():
-        for c in range(ct):
-            halo(0, c).wait_send()
+        wait_all(volume.at[rows - 1], halo_send.at[0])
 
     @pl.when(tile > 0)
     def _():
-        for c in range(ct):
-            halo(1, c).wait_send()
-
-    for j in range(1, slabs):
-        for side in range(2):
-            face_first(j, side).wait_send()
-        face_second(j).wait_send()
-        part_copy(1, j).wait_send()
-    for j in range(1, tiles_n):
-        part_copy(2, j).wait_send()
-
-    for j in range(1, slabs):
-        result_copy(depth_peer(j), me).wait_send()
-    for j in range(1, slabs):
-        result_copy(depth_peer(j), depth_peer(j)).wait_recv()
+        wait_all(volume.at[0], halo_send.at[1])
+
+    wait_all(face_in.at[pl.ds(0, others)], f1_send)
+    wait_all(face_out.at[pl.ds(0, others)], f2_send)
+    wait_all(part1.at[pl.ds(1, others)], m1_send)
+    wait_all(part2.at[pl.ds(1, tiles_n - 1)], m2_send)
+    wait_all(packed.at[pl.ds(0, others)], out_send)
+
+    wait_all(gathered.at[pl.ds(0, others)], out_recv)
 
     def composite(b, _):
         rs = pl.ds(pl.multiple_of(b * SUB, SUB), SUB)
@@ -532,18 +524,9 @@
                 pltpu.SMEM((slabs + 2,), jnp.int32),
                 dma((4,)),
                 dma((ct,)),
-                dma((2, ct)),
-                dma((2, ct)),
-                dma((slabs, 2)),
-                dma((slabs, 2)),
-                dma((slabs,)),
-                dma((slabs,)),
-                dma((slabs,)),
-                dma((slabs,)),
-                dma((tiles_n,)),
-                dma((tiles_n,)),
-                dma((slabs,)),
-                dma((slabs,)),
+                dma((2,)),
+                dma((2,)),
+                *[dma(())] * 11,
             ],
             compiler_params=pltpu.CompilerParams(
                 collective_id=0, has_side_effects=True, vmem_limit_bytes=48 << 20

time: 33.8 us -> 32.4 us (0.959)
  Pallas kernels: 33.1 us -> 31.6 us
    pallas_call x1, Pallas kernels: 33.1 us -> 31.6 us  [body(): pl.pallas_call(functools.partial(kernel, dims), out_shape=jax.ShapeDtypeS...]
where the time goes in v5:
time: 32.4 us; the launch traced here: 32.3 us
  Pallas kernels  31.6 us (98%)
  local copies, waits for them, and re-layouts  0.62 us (2%)
    pallas_call x1, Pallas kernels, body(): pl.pallas_call(functools.partial(kernel, dims), out_shape=jax.ShapeDtypeS...  31.6 us

profile of v5, /device:TPU:1, one launch (start us, length us, event | category | flops | bytes accessed | tf_op | source)
XLA Modules:
  0.0 32.3 jit_solution(7663754108745695122)
XLA Ops:
  0.0 31.6 %render.1 = f32[3,32,128]{2,1,0:T(8,128)S(1)} custom-call(f32[32,64,1024]{2,1,0:T(8,128)} %volume.1, s32[8]{0:T(128)} %place_hbm.1, s32[8]{0:T(128)} %index_hbm.1, f32[8]{0:T(128)} %extinct_hbm.1, f32[3,8]{1,0:T(4,128)} %color_hbm.1), custom_call_target="tpu_custom_call" | custom-call | tf_op jit(solution)/shard_map/render/pallas_call | solution.py:504
  31.6 0.6 %copy.7 = f32[3,32,128]{2,1,0:T(8,128)} copy(f32[3,32,128]{2,1,0:T(8,128)S(1)} %render.1) | data formatting | bytes 98304

commit v6 on v5

--- a/solution.py
+++ b/solution.py
@@ -267,7 +267,6 @@
     extremes = lax.fori_loop(0, run + 1, extremes_block, start)
     shade_inner(0)
     extremes = lax.fori_loop(run + 1, 2 * run + 1, extremes_block, extremes)
-    shade_inner(run)
     high, low = lax.fori_loop(2 * run + 1, ct, extremes_block, extremes)
     part1[0, 0:1, :] = jnp.max(functools.reduce(jnp.maximum, high), axis=0, keepdims=True)
     part1[0, 1:2, :] = -jnp.min(functools.reduce(jnp.minimum, low), axis=0, keepdims=True)
@@ -287,6 +286,7 @@
     for j in range(1, slabs):
         part_copy(1, j).start()
 
+    shade_inner(run)
     shade_inner(2 * run)
 
     others = slabs - 1
@@ -430,7 +430,7 @@
                 return tuple(out_carry)
 
             begin = tuple((full(1.0), (full(0.0),) * 3) for _ in range(pair))
-            done = lax.fori_loop(0, planes, step, begin, unroll=32)
+            done = lax.fori_loop(0, planes, step, begin, unroll=64)
             for k in range(pair):
                 for n in range(3):
                     result[owner, i * pair + k, n] = done[k][1][n]

time: 32.4 us -> 32 us (0.988)
  Pallas kernels: 31.6 us -> 31.2 us
    pallas_call x1, Pallas kernels: 31.6 us -> 31.2 us  [body(): pl.pallas_call(functools.partial(kernel, dims), out_shape=jax.ShapeDtypeS...]
where the time goes in v6:
time: 32 us; the launch traced here: 31.9 us
  Pallas kernels  31.2 us (98%)
  local copies, waits for them, and re-layouts  0.62 us (2%)
    pallas_call x1, Pallas kernels, body(): pl.pallas_call(functools.partial(kernel, dims), out_shape=jax.ShapeDtypeS...  31.2 us

profile of v6, /device:TPU:1, one launch (start us, length us, event | category | flops | bytes accessed | tf_op | source)
XLA Modules:
  0.0 31.9 jit_solution(1742535693860652626)
XLA Ops:
  0.0 31.2 %render.1 = f32[3,32,128]{2,1,0:T(8,128)S(1)} custom-call(f32[32,64,1024]{2,1,0:T(8,128)} %volume.1, s32[8]{0:T(128)} %place_hbm.1, s32[8]{0:T(128)} %index_hbm.1, f32[8]{0:T(128)} %extinct_hbm.1, f32[3,8]{1,0:T(4,128)} %color_hbm.1), custom_call_target="tpu_custom_call" | custom-call | tf_op jit(solution)/shard_map/render/pallas_call | solution.py:504
  31.2 0.6 %copy.7 = f32[3,32,128]{2,1,0:T(8,128)} copy(f32[3,32,128]{2,1,0:T(8,128)S(1)} %render.1) | data formatting | bytes 98304
